TPU v7x, 512 devices: a whole 4x4x16 slice. The times are simulated.
512 devices in a mesh: row: 16 (over y, x), col: 32 (over z, core).
Axes of the slice: x: 4, y: 4, z: 16, core: 2. Of those that a mesh axis runs over, the one named last changes fastest.
Arguments:
- tokens: bfloat16 [4096, 8192], P('row', 'col'), may hold values from -6 to 6
- w_in: bfloat16 [8192, 3, 8192], P('row', None, 'col'), may hold values from -0.0625 to 0.0625
- filt_in: float32 [7, 3, 8192], P(None, None, 'col'), may hold values from -2.4 to 2.4
- filt_mix: float32 [7, 8192], P(None, 'col'), may hold values from -2.4 to 2.4
Outputs:
- gated: bfloat16 [4096, 8192], P('row', 'col')
All inputs are finite; a program needn't handle non-finite values.
Results may differ from a plain program's by a relative error of at most 0.0064.
Values may be sent and summed in bfloat16 or wider, within the bound.
A program may use at most 64 MiB of HBM per device.

v0:
```python
import jax
import jax.numpy as jnp
from jax import lax
from jax.sharding import PartitionSpec as P


def passed_along(block, axis, distance):
    devices = range(lax.axis_size(axis))
    route = [(i - distance, i) for i in devices if i - distance in devices]
    return lax.ppermute(block, axis, route)


def taps(ext, filt, count):
    total = filt[0] * ext[6 : 6 + count]
    for shift_s in range(1, 7):
        total = total + filt[shift_s] * ext[6 - shift_s : 6 - shift_s + count]
    return total


def per_device(tokens, w_in, filt_in, filt_mix):
    rows = tokens.shape[0]
    cols = w_in.shape[2]
    strip = lax.all_gather(tokens, "col", axis=1, tiled=True)
    piece = lax.all_gather(w_in, "row", axis=0, tiled=True)
    flat_piece = piece.reshape(piece.shape[0], 3 * cols)
    summed = jnp.dot(strip, flat_piece, preferred_element_type=jnp.float32)
    proj = summed.astype(jnp.bfloat16).reshape(rows, 3, cols)
    starts_seq = lax.axis_index("row") == 0
    keep_f = jnp.where(starts_seq, 0.0, 1.0).astype(jnp.float32)
    rim = passed_along(proj[rows - 6 :], "row", 1)
    ext = jnp.concatenate([rim.astype(jnp.float32) * keep_f, proj.astype(jnp.float32)], axis=0)
    conv = taps(ext, filt_in, rows)
    prod = conv[:, 1] * conv[:, 2]
    prod_rim = passed_along(prod[rows - 6 :], "row", 1)
    ext_prod = jnp.concatenate([prod_rim * keep_f, prod], axis=0)
    mix = taps(ext_prod, filt_mix, rows)
    query = conv[:, 0]
    return (query * mix).astype(jnp.bfloat16)


def solution(mesh):
    return jax.shard_map(
        per_device,
        mesh=mesh,
        in_specs=(P("row", "col"), P("row", None, "col"), P(None, None, "col"), P(None, "col")),
        out_specs=P("row", "col"),
        check_vma=False,
    )
```

profile of v0, /device:TPU:8, one launch (start us, length us, event | category | flops | bytes accessed | tf_op | source)
XLA Modules:
  0.0 247.7 jit_solution(13775816980189097958)
XLA Ops:
  6.5 0.0 all-gather.3.cloned.1.call-start
  6.5 0.7 all-gather.3.cloned.1.call-update
  7.3 0.0 all-gather.5.cloned.1.call-start
  7.3 2.3 copy.8
  9.6 0.0 all-gather.5.cloned.1.call-update
  9.6 1.0 fusion.36
  10.7 83.2 %all-gather.3.cloned.1.call-done = bf16[256,8192]{1,0:T(8,128)(2,1)} async-done(((bf16[256,256]{1,0:T(8,128)(2,1)}), bf16[256,8192]{1,0:T(8,128)(2,1)}) %all-gather.3.cloned.1.call-update) | async-done | bytes 4194320 | tf_op jit(solution)/shard_map/all_gather | solution.py:23
  93.9 114.1 %all-gather.5.cloned.1.call-done = bf16[8192,3,256]{0,2,1:T(8,128)(2,1)} async-done(((bf16[512,3,256]{0,2,1:T(8,128)(2,1)}), bf16[8192,3,256]{0,2,1:T(8,128)(2,1)}) %all-gather.5.cloned.1.call-update) | async-done | bytes 12582928 | tf_op jit(solution)/shard_map/all_gather | solution.py:24
  208.0 0.0 copy-start
  208.0 9.3 %convolution_convert_fusion = bf16[256,768]{1,0:T(8,128)(2,1)S(1)} fusion(bf16[256,8192]{1,0:T(8,128)(2,1)} %all-gather.3.cloned.1.call-done, bf16[8192,768]{0,1:T(8,128)(2,1)} %bitcast.45), kind=kOutput, calls=%fused_computation.10 | convolution fusion | flops 3221422080 | bytes 17170432 | tf_op jit(solution)/shard_map/dot_general | solution.py:26
  217.3 0.2 copy.12
  217.5 2.2 collective-permute-start
  219.7 0.0 copy-done
  219.8 0.2 copy.9
  219.9 7.3 %collective-permute-done = bf16[6,3,256]{0,2,1:T(8,128)(2,1)S(1)} collective-permute-done((bf16[6,3,256]{0,2,1:T(8,128)(2,1)S(1)}, bf16[6,3,256]{0,2,1:T(8,128)(2,1)S(1)}, u32[]{:S(2)}, u32[]{:S(2)}) %collective-permute-start) | collective-permute-done | bytes 9248 | tf_op jit(solution)/shard_map/ppermute | solution.py:10
  227.3 2.7 %fusion.3 = f32[256,3,256]{0,2,1:T(8,128)S(1)} fusion(f32[256,3,256]{0,2,1:T(8,128)S(1)} %bitcast.35, f32[6,3,256]{0,2,1:T(8,128)S(1)} %convert_multiply_fusion, f32[3,256]{1,0:T(4,128)S(1)} %get-tuple-element.19, f32[3,256]{1,0:T(4,128)S(1)} %get-tuple-element.20, f32[3,256]{1,0:T(4,128)S(1)} %get-tuple-element.21, f32[3,256]{1,0:T(4,128)S(1)} %get-tuple-element.22, ...), kind=kLoop, calls=%fused_computation.19 | loop fusion | flops 3735552 | bytes 1612800 | tf_op jit(solution)/shard_map/add | solution.py:16
  230.1 0.1 slice_bitcast_fusion.1
  230.2 1.9 collective-permute-start.1
  232.1 7.0 %collective-permute-done.1 = f32[6,256]{0,1:T(8,128)S(1)} collective-permute-done((f32[6,256]{0,1:T(8,128)S(1)}, f32[6,256]{0,1:T(8,128)S(1)}, u32[]{:S(2)}, u32[]{:S(2)}) %collective-permute-start.1) | collective-permute-done | bytes 6176 | tf_op jit(solution)/shard_map/ppermute | solution.py:10
  239.2 0.9 fusion.22
  240.1 0.8 copy.11
  (10 shorter events, 0.1 us)
Async XLA Ops:
  6.5 87.4 %all-gather.3.cloned.1.call-start = ((), (), s32[]{:S(2)}) async-start(), calls=%async_computation | async-start | bytes 4325376 | tf_op jit(solution)/shard_map/all_gather | solution.py:23
  7.3 200.7 %all-gather.5.cloned.1.call-start = ((), (), s32[]{:S(2)}) async-start(), calls=%async_computation.1 | async-start | bytes 13369344 | tf_op jit(solution)/shard_map/all_gather | solution.py:24
  208.0 11.7 %copy-start = (f32[7,256]{1,0:T(8,128)S(1)}, f32[7,256]{1,0:T(8,128)}, u32[]{:S(2)}) copy-start(f32[7,256]{1,0:T(8,128)} %param.7) | copy-start | bytes 21508
  217.5 9.8 %collective-permute-start = (bf16[6,3,256]{0,2,1:T(8,128)(2,1)S(1)}, bf16[6,3,256]{0,2,1:T(8,128)(2,1)S(1)}, u32[]{:S(2)}, u32[]{:S(2)}) collective-permute-start(bf16[6,3,256]{0,2,1:T(8,128)(2,1)S(1)} %bitcast.36), channel_id=1, source_target_pairs={{0,32},{32,64},{64,96},{96,128},{128,160},{160,192},{192,224},{224... | collective-permute-start | bytes 27656 | tf_op jit(solution)/shard_map/ppermute | solution.py:10
  230.2 9.0 %collective-permute-start.1 = (f32[6,256]{0,1:T(8,128)S(1)}, f32[6,256]{0,1:T(8,128)S(1)}, u32[]{:S(2)}, u32[]{:S(2)}) collective-permute-start(f32[6,256]{0,1:T(8,128)S(1)} %slice_bitcast_fusion.1), channel_id=1, source_target_pairs={{0,32},{32,64},{64,96},{96,128},{128,160},{160,192},{192,224},{224... | collective-permute-start | bytes 18440 | tf_op jit(solution)/shard_map/ppermute | solution.py:10
Sparse Core Ops, SparseCore 0:
  9.4 84.4 all-gather.2
  96.9 111.0 all-gather.4
where the time goes:
time: 248 us
  waiting for transfers between devices  212 us (85%)
  between operations  13.5 us (5%)
  matrix products  9.31 us (4%)
  local copies, waits for them, and re-layouts  4.56 us (2%)
  starting transfers between devices  4.17 us (2%)
  other arithmetic  3.72 us (2%)
    all_gather x1, waiting for transfers between devices, per_device(): piece = lax.all_gather(w_in, 'row', axis=0, tiled=True)  114 us
    all_gather x1, waiting for transfers between devices, per_device(): strip = lax.all_gather(tokens, 'col', axis=1, tiled=True)  83.2 us
    ppermute x2, waiting for transfers between devices, passed_along(): return lax.ppermute(block, axis, route)  14.3 us
    dot_general x1, matrix products, per_device(): summed = jnp.dot(strip, flat_piece, preferred_element_type=jnp.float32)  9.31 us
  transfers between devices with their start and end apart: 4, of which 4 were waited for; matrix products, arithmetic and copies ran while one was open for 1% of the time, Pallas kernels for 0%

commit v1 on v0

--- a/solution.py
+++ b/solution.py
@@ -21,7 +21,16 @@
     rows = tokens.shape[0]
     cols = w_in.shape[2]
     strip = lax.all_gather(tokens, "col", axis=1, tiled=True)
-    piece = lax.all_gather(w_in, "row", axis=0, tiled=True)
+    ways = lax.axis_size("row")
+    up = [(d, (d + 1) % ways) for d in range(ways)]
+    down = [(d, (d - 1) % ways) for d in range(ways)]
+    earlier, later = ([w_in], [w_in])
+    for _ in range(ways // 2):
+        earlier.append(lax.ppermute(earlier[-1], "row", up))
+    for _ in range((ways - 1) // 2):
+        later.append(lax.ppermute(later[-1], "row", down))
+    line = jnp.concatenate([*earlier[::-1], *later[1:]], axis=0)
+    piece = jnp.roll(line, (lax.axis_index("row") - ways // 2) * w_in.shape[0], axis=0)
     flat_piece = piece.reshape(piece.shape[0], 3 * cols)
     summed = jnp.dot(strip, flat_piece, preferred_element_type=jnp.float32)
     proj = summed.astype(jnp.bfloat16).reshape(rows, 3, cols)

time: 248 us -> 240 us (0.968)
  the two profiles are of different devices: /device:TPU:8 before, /device:TPU:34 now
where the time goes in v1:
time: 240 us; the launch traced here: 238 us
  waiting for transfers between devices  111 us (46%)
  starting transfers between devices  68.4 us (29%)
  local copies, waits for them, and re-layouts  34.2 us (14%)
  between operations  14.1 us (6%)
  matrix products  9.2 us (4%)
    ppermute x8, waiting for transfers between devices, per_device(): earlier.append(lax.ppermute(earlier[-1], 'row', up))  102 us
    ppermute x7, starting transfers between devices, per_device(): later.append(lax.ppermute(later[-1], 'row', down))  46.3 us
    unnamed x50, local copies, waits for them, and re-layouts  27.3 us
    ppermute x8, starting transfers between devices, per_device(): earlier.append(lax.ppermute(earlier[-1], 'row', up))  18.2 us
    ppermute x2, waiting for transfers between devices, passed_along(): return lax.ppermute(block, axis, route)  9.28 us
    dot_general x1, matrix products, per_device(): summed = jnp.dot(strip, flat_piece, preferred_element_type=jnp.float32)  9.2 us
    dynamic_slice x1, local copies, waits for them, and re-layouts, per_device(): jnp.roll(line, (lax.axis_index('row') - ways // 2) * w_in.shape[0], axis=0)  5.33 us
  transfers between devices with their start and end apart: 18, of which 10 were waited for; matrix products, arithmetic and copies ran while one was open for 13% of the time, Pallas kernels for 0%

profile of v1, /device:TPU:34, one launch (start us, length us, event | category | flops | bytes accessed | tf_op | source)
XLA Modules:
  0.0 238.4 jit_solution(3290881955986103635)
XLA Ops:
  6.5 1.4 copy.8
  7.9 3.4 %collective-permute-start = (bf16[512,3,256]{0,2,1:T(8,128)(2,1)S(1)}, bf16[512,3,256]{0,2,1:T(8,128)(2,1)S(1)}, u32[]{:S(2)}, u32[]{:S(2)}) collective-permute-start(bf16[512,3,256]{0,2,1:T(8,128)(2,1)S(1)} %copy.8), channel_id=1, source_target_pairs={{0,32},{32,64},{64,96},{96,128},{128,160},{160,192},{192,224},{224... | collective-permute-start | bytes 2359304 | tf_op jit(solution)/shard_map/ppermute | solution.py:29
  11.4 17.8 %collective-permute-done = bf16[512,3,256]{0,2,1:T(8,128)(2,1)S(1)} collective-permute-done((bf16[512,3,256]{0,2,1:T(8,128)(2,1)S(1)}, bf16[512,3,256]{0,2,1:T(8,128)(2,1)S(1)}, u32[]{:S(2)}, u32[]{:S(2)}) %collective-permute-start) | collective-permute-done | bytes 786464 | tf_op jit(solution)/shard_map/ppermute | solution.py:29
  29.1 3.4 %collective-permute-start.1 = (bf16[512,3,256]{0,2,1:T(8,128)(2,1)S(1)}, bf16[512,3,256]{0,2,1:T(8,128)(2,1)S(1)}, u32[]{:S(2)}, u32[]{:S(2)}) collective-permute-start(bf16[512,3,256]{0,2,1:T(8,128)(2,1)S(1)} %collective-permute-done), channel_id=1, source_target_pairs={{0,32},{32,64},{64,96},{96,128},{128,160},{160,192},{192,224},{224... | collective-permute-start | bytes 2359304 | tf_op jit(solution)/shard_map/ppermute | solution.py:29
  32.5 4.4 %collective-permute-start.8 = (bf16[512,3,256]{0,2,1:T(8,128)(2,1)S(1)}, bf16[512,3,256]{0,2,1:T(8,128)(2,1)S(1)}, u32[]{:S(2)}, u32[]{:S(2)}) collective-permute-start(bf16[512,3,256]{0,2,1:T(8,128)(2,1)S(1)} %copy.8), channel_id=1, source_target_pairs={{0,480},{32,0},{64,32},{96,64},{128,96},{160,128},{192,160},{224,1... | collective-permute-start | bytes 2359304 | tf_op jit(solution)/shard_map/ppermute | solution.py:31
  37.0 14.9 %collective-permute-done.1 = bf16[512,3,256]{0,2,1:T(8,128)(2,1)S(1)} collective-permute-done((bf16[512,3,256]{0,2,1:T(8,128)(2,1)S(1)}, bf16[512,3,256]{0,2,1:T(8,128)(2,1)S(1)}, u32[]{:S(2)}, u32[]{:S(2)}) %collective-permute-start.1) | collective-permute-done | bytes 786464 | tf_op jit(solution)/shard_map/ppermute | solution.py:29
  51.9 1.9 collective-permute-start.2
  53.8 7.0 %collective-permute-start.9 = (bf16[512,3,256]{0,2,1:T(8,128)(2,1)S(1)}, bf16[512,3,256]{0,2,1:T(8,128)(2,1)}, u32[]{:S(2)}, u32[]{:S(2)}) collective-permute-start(bf16[512,3,256]{0,2,1:T(8,128)(2,1)S(1)} %collective-permute-done.8), channel_id=1, source_target_pairs={{0,480},{32,0},{64,32},{96,64},{128,96},{160,128},{192,160},{224,1... | collective-permute-start | bytes 2359304 | tf_op jit(solution)/shard_map/ppermute | solution.py:31
  60.8 14.0 %collective-permute-done.2 = bf16[512,3,256]{0,2,1:T(8,128)(2,1)S(1)} collective-permute-done((bf16[512,3,256]{0,2,1:T(8,128)(2,1)S(1)}, bf16[512,3,256]{0,2,1:T(8,128)(2,1)S(1)}, u32[]{:S(2)}, u32[]{:S(2)}) %collective-permute-start.2) | collective-permute-done | bytes 786464 | tf_op jit(solution)/shard_map/ppermute | solution.py:29
  74.7 1.9 collective-permute-start.3
  76.7 7.0 %collective-permute-start.10 = (bf16[512,3,256]{0,2,1:T(8,128)(2,1)}, bf16[512,3,256]{0,2,1:T(8,128)(2,1)}, u32[]{:S(2)}, u32[]{:S(2)}) collective-permute-start(bf16[512,3,256]{0,2,1:T(8,128)(2,1)} %collective-permute-done.9), channel_id=1, source_target_pairs={{0,480},{32,0},{64,32},{96,64},{128,96},{160,128},{192,160},{224,1... | collective-permute-start | bytes 2359304 | tf_op jit(solution)/shard_map/ppermute | solution.py:31
  83.6 13.1 %collective-permute-done.3 = bf16[512,3,256]{0,2,1:T(8,128)(2,1)} collective-permute-done((bf16[512,3,256]{0,2,1:T(8,128)(2,1)S(1)}, bf16[512,3,256]{0,2,1:T(8,128)(2,1)}, u32[]{:S(2)}, u32[]{:S(2)}) %collective-permute-start.3) | collective-permute-done | bytes 786464 | tf_op jit(solution)/shard_map/ppermute | solution.py:29
  96.8 1.9 collective-permute-start.4
  98.7 7.0 %collective-permute-start.11 = (bf16[512,3,256]{0,2,1:T(8,128)(2,1)}, bf16[512,3,256]{0,2,1:T(8,128)(2,1)S(1)}, u32[]{:S(2)}, u32[]{:S(2)}) collective-permute-start(bf16[512,3,256]{0,2,1:T(8,128)(2,1)} %collective-permute-done.10), channel_id=1, source_target_pairs={{0,480},{32,0},{64,32},{96,64},{128,96},{160,128},{192,160},{224,1... | collective-permute-start | bytes 2359304 | tf_op jit(solution)/shard_map/ppermute | solution.py:31
  105.7 12.4 %collective-permute-done.4 = bf16[512,3,256]{0,2,1:T(8,128)(2,1)} collective-permute-done((bf16[512,3,256]{0,2,1:T(8,128)(2,1)}, bf16[512,3,256]{0,2,1:T(8,128)(2,1)}, u32[]{:S(2)}, u32[]{:S(2)}) %collective-permute-start.4) | collective-permute-done | bytes 786464 | tf_op jit(solution)/shard_map/ppermute | solution.py:29
  118.1 1.9 collective-permute-start.5
  120.1 0.9 copy-done.2
  120.9 7.0 %collective-permute-start.12 = (bf16[512,3,256]{0,2,1:T(8,128)(2,1)S(1)}, bf16[512,3,256]{0,2,1:T(8,128)(2,1)}, u32[]{:S(2)}, u32[]{:S(2)}) collective-permute-start(bf16[512,3,256]{0,2,1:T(8,128)(2,1)S(1)} %collective-permute-done.11), channel_id=1, source_target_pairs={{0,480},{32,0},{64,32},{96,64},{128,96},{160,128},{192,160},{224,1... | collective-permute-start | bytes 2359304 | tf_op jit(solution)/shard_map/ppermute | solution.py:31
  127.9 10.5 %collective-permute-done.5 = bf16[512,3,256]{0,2,1:T(8,128)(2,1)S(1)} collective-permute-done((bf16[512,3,256]{0,2,1:T(8,128)(2,1)}, bf16[512,3,256]{0,2,1:T(8,128)(2,1)S(1)}, u32[]{:S(2)}, u32[]{:S(2)}) %collective-permute-start.5) | collective-permute-done | bytes 786464 | tf_op jit(solution)/shard_map/ppermute | solution.py:29
  138.4 1.9 collective-permute-start.6
  140.4 7.0 %collective-permute-start.13 = (bf16[512,3,256]{0,2,1:T(8,128)(2,1)}, bf16[512,3,256]{0,2,1:T(8,128)(2,1)}, u32[]{:S(2)}, u32[]{:S(2)}) collective-permute-start(bf16[512,3,256]{0,2,1:T(8,128)(2,1)} %collective-permute-done.12), channel_id=1, source_target_pairs={{0,480},{32,0},{64,32},{96,64},{128,96},{160,128},{192,160},{224,1... | collective-permute-start | bytes 2359304 | tf_op jit(solution)/shard_map/ppermute | solution.py:31
  147.4 10.4 %collective-permute-done.6 = bf16[512,3,256]{0,2,1:T(8,128)(2,1)} collective-permute-done((bf16[512,3,256]{0,2,1:T(8,128)(2,1)S(1)}, bf16[512,3,256]{0,2,1:T(8,128)(2,1)}, u32[]{:S(2)}, u32[]{:S(2)}) %collective-permute-start.6) | collective-permute-done | bytes 786464 | tf_op jit(solution)/shard_map/ppermute | solution.py:29
  157.7 1.9 collective-permute-start.7
  159.6 1.0 fusion.36
  160.8 7.1 %collective-permute-start.14 = (bf16[512,3,256]{0,2,1:T(8,128)(2,1)}, bf16[512,3,256]{0,2,1:T(8,128)(2,1)S(1)}, u32[]{:S(2)}, u32[]{:S(2)}) collective-permute-start(bf16[512,3,256]{0,2,1:T(8,128)(2,1)} %collective-permute-done.13), channel_id=1, source_target_pairs={{0,480},{32,0},{64,32},{96,64},{128,96},{160,128},{192,160},{224,1... | collective-permute-start | bytes 2359304 | tf_op jit(solution)/shard_map/ppermute | solution.py:31
  167.9 8.4 %collective-permute-done.7 = bf16[512,3,256]{0,2,1:T(8,128)(2,1)} collective-permute-done((bf16[512,3,256]{0,2,1:T(8,128)(2,1)}, bf16[512,3,256]{0,2,1:T(8,128)(2,1)}, u32[]{:S(2)}, u32[]{:S(2)}) %collective-permute-start.7) | collective-permute-done | bytes 786464 | tf_op jit(solution)/shard_map/ppermute | solution.py:29
  176.3 1.2 constant_dynamic-update-slice_fusion.31
  177.5 1.2 constant_dynamic-update-slice_fusion.30
  178.8 1.3 constant_dynamic-update-slice_fusion.29
  180.1 1.2 constant_dynamic-update-slice_fusion.28
  181.3 1.2 constant_dynamic-update-slice_fusion.27
  182.6 1.2 constant_dynamic-update-slice_fusion.26
  183.8 0.1 constant_dynamic-update-slice_fusion.25
  184.0 0.1 constant_dynamic-update-slice_fusion.24
  184.1 0.1 constant_dynamic-update-slice_fusion.23
  184.2 0.1 constant_dynamic-update-slice_fusion.22
  184.3 1.2 constant_dynamic-update-slice_fusion.21
  185.6 1.2 constant_dynamic-update-slice_fusion.20
  186.8 1.2 constant_dynamic-update-slice_fusion.19
  188.1 1.2 constant_dynamic-update-slice_fusion.18
  189.3 1.2 constant_dynamic-update-slice_fusion.17
  190.7 1.2 constant_dynamic-update-slice_fusion.15
  192.0 1.2 constant_dynamic-update-slice_fusion.14
  193.3 1.2 constant_dynamic-update-slice_fusion.12
  194.6 1.2 constant_dynamic-update-slice_fusion.11
  196.0 0.1 constant_dynamic-update-slice_fusion.9
  196.1 0.1 constant_dynamic-update-slice_fusion.8
  196.2 0.1 constant_dynamic-update-slice_fusion.7
  196.3 0.1 constant_dynamic-update-slice_fusion.6
  196.4 1.2 constant_dynamic-update-slice_fusion.5
  197.7 1.2 constant_dynamic-update-slice_fusion.4
  199.1 1.2 constant_dynamic-update-slice_fusion.2
  200.3 1.2 constant_dynamic-update-slice_fusion.1
  201.7 5.3 %constant_dynamic-slice_fusion = bf16[8192,3,256]{0,2,1:T(8,128)(2,1)} fusion(bf16[16384,3,256]{0,2,1:T(8,128)(2,1)S(1)} %constant_dynamic-update-slice_fusion, s32[]{:T(128)S(6)} %select_n.18), kind=kLoop, calls=%fused_computation.99 | loop fusion | bytes 25165828 | tf_op jit(solution)/shard_map/jit(_roll_dynamic)/dynamic_slice | solution.py:33
  207.0 9.2 %convolution_convert_fusion = bf16[768,256]{1,0:T(8,128)(2,1)S(1)} fusion(bf16[8192,768]{0,1:T(8,128)(2,1)} %bitcast.38, bf16[256,8192]{1,0:T(8,128)(2,1)} %all-gather.2.cloned.1.call-done), kind=kOutput, calls=%fused_computation.5 | convolution fusion | flops 3221422080 | bytes 17170432 | tf_op jit(solution)/shard_map/dot_general | solution.py:35
  216.2 0.1 slice.132
  216.4 0.1 copy.13
  216.5 1.9 collective-permute-start.15
  218.5 0.2 copy.12
  218.6 5.7 %collective-permute-done.15 = bf16[6,3,256]{2,0,1:T(8,128)(2,1)S(1)} collective-permute-done((bf16[6,3,256]{2,0,1:T(8,128)(2,1)S(1)}, bf16[6,3,256]{2,0,1:T(8,128)(2,1)S(1)}, u32[]{:S(2)}, u32[]{:S(2)}) %collective-permute-start.15) | collective-permute-done | bytes 9248 | tf_op jit(solution)/shard_map/ppermute | solution.py:10
  224.4 0.7 fusion.3
  225.1 1.9 collective-permute-start.16
  227.0 3.6 %collective-permute-done.16 = f32[6,256]{1,0:T(8,128)S(1)} collective-permute-done((f32[6,256]{1,0:T(8,128)S(1)}, f32[6,256]{1,0:T(8,128)S(1)}, u32[]{:S(2)}, u32[]{:S(2)}) %collective-permute-start.16) | collective-permute-done | bytes 6176 | tf_op jit(solution)/shard_map/ppermute | solution.py:10
  230.6 0.9 fusion.22
  (38 shorter events, 0.7 us)
Async XLA Ops:
  6.5 200.5 %all-gather.2.cloned.1.call-start = ((), (), s32[]{:S(2)}) async-start(), calls=%async_computation | async-start | bytes 4325376 | tf_op jit(solution)/shard_map/all_gather | solution.py:23
  7.9 21.2 %collective-permute-start = (bf16[512,3,256]{0,2,1:T(8,128)(2,1)S(1)}, bf16[512,3,256]{0,2,1:T(8,128)(2,1)S(1)}, u32[]{:S(2)}, u32[]{:S(2)}) collective-permute-start(bf16[512,3,256]{0,2,1:T(8,128)(2,1)S(1)} %copy.8), channel_id=1, source_target_pairs={{0,32},{32,64},{64,96},{96,128},{128,160},{160,192},{192,224},{224... | collective-permute-start | bytes 2359304 | tf_op jit(solution)/shard_map/ppermute | solution.py:29
  29.1 22.7 %collective-permute-start.1 = (bf16[512,3,256]{0,2,1:T(8,128)(2,1)S(1)}, bf16[512,3,256]{0,2,1:T(8,128)(2,1)S(1)}, u32[]{:S(2)}, u32[]{:S(2)}) collective-permute-start(bf16[512,3,256]{0,2,1:T(8,128)(2,1)S(1)} %collective-permute-done), channel_id=1, source_target_pairs={{0,32},{32,64},{64,96},{96,128},{128,160},{160,192},{192,224},{224... | collective-permute-start | bytes 2359304 | tf_op jit(solution)/shard_map/ppermute | solution.py:29
  32.5 21.3 %collective-permute-start.8 = (bf16[512,3,256]{0,2,1:T(8,128)(2,1)S(1)}, bf16[512,3,256]{0,2,1:T(8,128)(2,1)S(1)}, u32[]{:S(2)}, u32[]{:S(2)}) collective-permute-start(bf16[512,3,256]{0,2,1:T(8,128)(2,1)S(1)} %copy.8), channel_id=1, source_target_pairs={{0,480},{32,0},{64,32},{96,64},{128,96},{160,128},{192,160},{224,1... | collective-permute-start | bytes 2359304 | tf_op jit(solution)/shard_map/ppermute | solution.py:31
  51.9 22.9 %collective-permute-start.2 = (bf16[512,3,256]{0,2,1:T(8,128)(2,1)S(1)}, bf16[512,3,256]{0,2,1:T(8,128)(2,1)S(1)}, u32[]{:S(2)}, u32[]{:S(2)}) collective-permute-start(bf16[512,3,256]{0,2,1:T(8,128)(2,1)S(1)} %collective-permute-done.1), channel_id=1, source_target_pairs={{0,32},{32,64},{64,96},{96,128},{128,160},{160,192},{192,224},{224... | collective-permute-start | bytes 2359304 | tf_op jit(solution)/shard_map/ppermute | solution.py:29
  53.8 22.9 %collective-permute-start.9 = (bf16[512,3,256]{0,2,1:T(8,128)(2,1)S(1)}, bf16[512,3,256]{0,2,1:T(8,128)(2,1)}, u32[]{:S(2)}, u32[]{:S(2)}) collective-permute-start(bf16[512,3,256]{0,2,1:T(8,128)(2,1)S(1)} %collective-permute-done.8), channel_id=1, source_target_pairs={{0,480},{32,0},{64,32},{96,64},{128,96},{160,128},{192,160},{224,1... | collective-permute-start | bytes 2359304 | tf_op jit(solution)/shard_map/ppermute | solution.py:31
  74.7 1.9 copy-start
  74.7 22.1 %collective-permute-start.3 = (bf16[512,3,256]{0,2,1:T(8,128)(2,1)S(1)}, bf16[512,3,256]{0,2,1:T(8,128)(2,1)}, u32[]{:S(2)}, u32[]{:S(2)}) collective-permute-start(bf16[512,3,256]{0,2,1:T(8,128)(2,1)S(1)} %collective-permute-done.2), channel_id=1, source_target_pairs={{0,32},{32,64},{64,96},{96,128},{128,160},{160,192},{192,224},{224... | collective-permute-start | bytes 2359304 | tf_op jit(solution)/shard_map/ppermute | solution.py:29
  76.7 22.1 %collective-permute-start.10 = (bf16[512,3,256]{0,2,1:T(8,128)(2,1)}, bf16[512,3,256]{0,2,1:T(8,128)(2,1)}, u32[]{:S(2)}, u32[]{:S(2)}) collective-permute-start(bf16[512,3,256]{0,2,1:T(8,128)(2,1)} %collective-permute-done.9), channel_id=1, source_target_pairs={{0,480},{32,0},{64,32},{96,64},{128,96},{160,128},{192,160},{224,1... | collective-permute-start | bytes 2359304 | tf_op jit(solution)/shard_map/ppermute | solution.py:31
  96.8 21.3 %collective-permute-start.4 = (bf16[512,3,256]{0,2,1:T(8,128)(2,1)}, bf16[512,3,256]{0,2,1:T(8,128)(2,1)}, u32[]{:S(2)}, u32[]{:S(2)}) collective-permute-start(bf16[512,3,256]{0,2,1:T(8,128)(2,1)} %collective-permute-done.3), channel_id=1, source_target_pairs={{0,32},{32,64},{64,96},{96,128},{128,160},{160,192},{192,224},{224... | collective-permute-start | bytes 2359304 | tf_op jit(solution)/shard_map/ppermute | solution.py:29
  98.7 21.3 %collective-permute-start.11 = (bf16[512,3,256]{0,2,1:T(8,128)(2,1)}, bf16[512,3,256]{0,2,1:T(8,128)(2,1)S(1)}, u32[]{:S(2)}, u32[]{:S(2)}) collective-permute-start(bf16[512,3,256]{0,2,1:T(8,128)(2,1)} %collective-permute-done.10), channel_id=1, source_target_pairs={{0,480},{32,0},{64,32},{96,64},{128,96},{160,128},{192,160},{224,1... | collective-permute-start | bytes 2359304 | tf_op jit(solution)/shard_map/ppermute | solution.py:31
  118.1 20.3 %collective-permute-start.5 = (bf16[512,3,256]{0,2,1:T(8,128)(2,1)}, bf16[512,3,256]{0,2,1:T(8,128)(2,1)S(1)}, u32[]{:S(2)}, u32[]{:S(2)}) collective-permute-start(bf16[512,3,256]{0,2,1:T(8,128)(2,1)} %collective-permute-done.4), channel_id=1, source_target_pairs={{0,32},{32,64},{64,96},{96,128},{128,160},{160,192},{192,224},{224... | collective-permute-start | bytes 2359304 | tf_op jit(solution)/shard_map/ppermute | solution.py:29
  120.1 0.9 copy-start.2
  120.9 19.4 %collective-permute-start.12 = (bf16[512,3,256]{0,2,1:T(8,128)(2,1)S(1)}, bf16[512,3,256]{0,2,1:T(8,128)(2,1)}, u32[]{:S(2)}, u32[]{:S(2)}) collective-permute-start(bf16[512,3,256]{0,2,1:T(8,128)(2,1)S(1)} %collective-permute-done.11), channel_id=1, source_target_pairs={{0,480},{32,0},{64,32},{96,64},{128,96},{160,128},{192,160},{224,1... | collective-permute-start | bytes 2359304 | tf_op jit(solution)/shard_map/ppermute | solution.py:31
  138.4 1.9 copy-start.4
  138.4 19.3 %collective-permute-start.6 = (bf16[512,3,256]{0,2,1:T(8,128)(2,1)S(1)}, bf16[512,3,256]{0,2,1:T(8,128)(2,1)}, u32[]{:S(2)}, u32[]{:S(2)}) collective-permute-start(bf16[512,3,256]{0,2,1:T(8,128)(2,1)S(1)} %collective-permute-done.5), channel_id=1, source_target_pairs={{0,32},{32,64},{64,96},{96,128},{128,160},{160,192},{192,224},{224... | collective-permute-start | bytes 2359304 | tf_op jit(solution)/shard_map/ppermute | solution.py:29
  140.4 20.4 %collective-permute-start.13 = (bf16[512,3,256]{0,2,1:T(8,128)(2,1)}, bf16[512,3,256]{0,2,1:T(8,128)(2,1)}, u32[]{:S(2)}, u32[]{:S(2)}) collective-permute-start(bf16[512,3,256]{0,2,1:T(8,128)(2,1)} %collective-permute-done.12), channel_id=1, source_target_pairs={{0,480},{32,0},{64,32},{96,64},{128,96},{160,128},{192,160},{224,1... | collective-permute-start | bytes 2359304 | tf_op jit(solution)/shard_map/ppermute | solution.py:31
  157.7 18.6 %collective-permute-start.7 = (bf16[512,3,256]{0,2,1:T(8,128)(2,1)}, bf16[512,3,256]{0,2,1:T(8,128)(2,1)}, u32[]{:S(2)}, u32[]{:S(2)}) collective-permute-start(bf16[512,3,256]{0,2,1:T(8,128)(2,1)} %collective-permute-done.6), channel_id=1, source_target_pairs={{0,32},{32,64},{64,96},{96,128},{128,160},{160,192},{192,224},{224... | collective-permute-start | bytes 2359304 | tf_op jit(solution)/shard_map/ppermute | solution.py:29
  160.7 32.5 %copy-start.5 = (bf16[512,3,256]{0,2,1:T(8,128)(2,1)S(1)}, bf16[512,3,256]{0,2,1:T(8,128)(2,1)}, u32[]{:S(2)}) copy-start(bf16[512,3,256]{0,2,1:T(8,128)(2,1)} %copy-done.4) | copy-start | bytes 2359300
  160.7 35.1 %copy-start.1 = (bf16[512,3,256]{0,2,1:T(8,128)(2,1)S(1)}, bf16[512,3,256]{0,2,1:T(8,128)(2,1)}, u32[]{:S(2)}) copy-start(bf16[512,3,256]{0,2,1:T(8,128)(2,1)} %copy-done) | copy-start | bytes 2359300
  160.7 38.2 %copy-start.3 = (bf16[512,3,256]{0,2,1:T(8,128)(2,1)S(1)}, bf16[512,3,256]{0,2,1:T(8,128)(2,1)}, u32[]{:S(2)}) copy-start(bf16[512,3,256]{0,2,1:T(8,128)(2,1)} %copy-done.2) | copy-start | bytes 2359300
  160.8 29.8 %collective-permute-start.14 = (bf16[512,3,256]{0,2,1:T(8,128)(2,1)}, bf16[512,3,256]{0,2,1:T(8,128)(2,1)S(1)}, u32[]{:S(2)}, u32[]{:S(2)}) collective-permute-start(bf16[512,3,256]{0,2,1:T(8,128)(2,1)} %collective-permute-done.13), channel_id=1, source_target_pairs={{0,480},{32,0},{64,32},{96,64},{128,96},{160,128},{192,160},{224,1... | collective-permute-start | bytes 2359304 | tf_op jit(solution)/shard_map/ppermute | solution.py:31
  201.6 16.8 %copy-start.6 = (f32[7,256]{1,0:T(8,128)S(1)}, f32[7,256]{1,0:T(8,128)}, u32[]{:S(2)}) copy-start(f32[7,256]{1,0:T(8,128)} %param.7) | copy-start | bytes 21508
  216.5 7.9 %collective-permute-start.15 = (bf16[6,3,256]{2,0,1:T(8,128)(2,1)S(1)}, bf16[6,3,256]{2,0,1:T(8,128)(2,1)S(1)}, u32[]{:S(2)}, u32[]{:S(2)}) collective-permute-start(bf16[6,3,256]{2,0,1:T(8,128)(2,1)S(1)} %copy.13), channel_id=1, source_target_pairs={{0,32},{32,64},{64,96},{96,128},{128,160},{160,192},{192,224},{224... | collective-permute-start | bytes 27656 | tf_op jit(solution)/shard_map/ppermute | solution.py:10
  225.1 5.5 %collective-permute-start.16 = (f32[6,256]{1,0:T(8,128)S(1)}, f32[6,256]{1,0:T(8,128)S(1)}, u32[]{:S(2)}, u32[]{:S(2)}) collective-permute-start(f32[6,256]{1,0:T(8,128)S(1)} %slice_bitcast_fusion.1), channel_id=1, source_target_pairs={{0,32},{32,64},{64,96},{96,128},{128,160},{160,192},{192,224},{224... | collective-permute-start | bytes 18440 | tf_op jit(solution)/shard_map/ppermute | solution.py:10
Sparse Core Ops, SparseCore 0:
  98.9 87.7 all-gather.1
